TPU v7x, 256 devices: a whole 4x4x8 slice. The times are simulated.
256 devices in a mesh: pair: 32 (over z_lo, y, x), sector: 8 (over z_hi, core).
Axes of the slice: x: 4, y: 4, z: 8 (z_hi: 4, z_lo: 2; z = z_hi * 2 + z_lo), core: 2. Of those that a mesh axis runs over, the one named last changes fastest.
Arguments:
- wavefunction: float32 [8, 512, 512], P('sector', 'pair'), may hold values from -6 to 6
- preconditioner: float32 [8, 512, 512], P('sector', 'pair'), may hold values from 0.5 to 4
- left_ops: float32 [96, 8, 512, 512], P('pair', 'sector'), may hold values from -0.25 to 0.25
- right_ops: float32 [96, 8, 512, 512], P('pair', 'sector'), may hold values from -0.01953125 to 0.01953125
- charges: int32 [96], P('pair'), may hold values from 0 to 2
- coupling: int32 [8, 3], P('sector'), may hold values 0 or 1
Outputs:
- new_state: float32 [8, 512, 512], P('sector', 'pair')
- new_image: float32 [8, 512, 512], P('sector', 'pair')
- energies: float32 [2], replicated
All inputs are finite; a program needn't handle non-finite values. No bound on the sum of `coupling` on one device may be relied on, other than what follows from the above.
Results may differ from a plain program's by a relative error of at most 0.0003.
Values sent between devices are 32-bit elements; how exact they have to be, the bound alone decides.
A program may use at most 64 MiB of HBM per device.

v0:
```python
import math
import jax
import jax.numpy as jnp
from jax import lax
from jax.sharding import Mesh
from jax.sharding import PartitionSpec as P

SECTOR = ("sector_0", "sector_1")
PAIR = ("pair_0", "pair_1", "pair_2")
PAIR_SECTOR = ("pair_0", "pair_1", "pair_2", "sector_0", "sector_1")
highest = lax.Precision.HIGHEST


def shifted(block, axis, distance):
    devices = range(lax.axis_size(axis))
    route = [((i - distance) % len(devices), i) for i in devices]
    return lax.ppermute(block, axis, route)


def side_by_side(arrays, axis, dim, along):
    widths = [a.shape[along] for a in arrays]
    both = jnp.concatenate(arrays, axis=along)
    out = lax.all_gather(both, axis, axis=dim, tiled=True)
    return tuple(jnp.split(out, [sum(widths[:k]) for k in range(1, len(widths))], axis=along))


def cut_along(value, dim, peers):
    lengths = value.shape
    blocks = value.reshape(*lengths[:dim], peers, lengths[dim] // peers, *lengths[dim + 1 :])
    return jnp.moveaxis(blocks, dim, 0)


def sum_at_owner(value, axis, dim):
    peers = lax.axis_size(axis)
    blocks = lax.all_to_all(cut_along(value, dim, peers), axis, 0, 0, tiled=True)
    return jnp.sum(blocks, axis=0)


def by_axis(value, axes):
    for axis in axes:
        value = lax.psum(value, axis)
    return value


def product(first, second):
    return jnp.dot(first, second, precision=highest, preferred_element_type=jnp.float32)


def sigma_apply(vector, left_ops, right_ops, charges, coupling):
    lower_rows = shifted(vector, SECTOR, 1)
    upper_rows = shifted(vector, SECTOR, -1)
    gathered = side_by_side((lower_rows, vector, upper_rows), PAIR, 1, 0)
    stacked = jnp.concatenate(gathered, axis=0)
    own_block = stacked[1]
    targets = jnp.zeros_like(stacked)
    for which_pair in range(left_ops.shape[0]):
        left_block = left_ops[which_pair, 0]
        right_block = right_ops[which_pair, 0]
        charge_slot = charges[which_pair]
        allowed = lax.dynamic_index_in_dim(coupling[0], charge_slot, 0, keepdims=False).astype(
            jnp.float32
        )
        source_block = lax.dynamic_index_in_dim(stacked, charge_slot, 0, keepdims=False)
        forward = product(product(left_block, own_block), right_block.T)
        backward = product(product(left_block.T, source_block), right_block)
        current = lax.dynamic_index_in_dim(targets, charge_slot, 0, keepdims=False)
        targets = lax.dynamic_update_index_in_dim(
            targets, current + allowed * forward, charge_slot, 0
        )
        targets = targets.at[1].add(allowed * backward)
    from_below = shifted(targets[2], SECTOR, 1)
    from_above = shifted(targets[0], SECTOR, -1)
    combined = targets[1] + from_below + from_above
    return sum_at_owner(combined[None], PAIR, 1)


def per_device(wavefunction, preconditioner, left_ops, right_ops, charges, coupling):
    first_image = sigma_apply(wavefunction, left_ops, right_ops, charges, coupling)
    norm_sq, correlation = (
        by_axis(jnp.sum(wavefunction * wavefunction), PAIR_SECTOR),
        by_axis(jnp.sum(wavefunction * first_image), PAIR_SECTOR),
    )
    theta = correlation / norm_sq
    inverse = lax.rsqrt(norm_sq)
    vector = wavefunction * inverse
    image = first_image * inverse
    residual = image - theta * vector
    correction = residual / preconditioner
    along, squared = (
        by_axis(jnp.sum(vector * correction), PAIR_SECTOR),
        by_axis(jnp.sum(correction * correction), PAIR_SECTOR),
    )
    orthogonal = correction - along * vector
    length_sq = squared - along * along
    basis = orthogonal * lax.rsqrt(length_sq + 1e-30)
    second_image = sigma_apply(basis, left_ops, right_ops, charges, coupling)
    corner, cross = (
        by_axis(jnp.sum(basis * second_image), PAIR_SECTOR),
        by_axis(jnp.sum(vector * second_image), PAIR_SECTOR),
    )
    half = (theta - corner) / 2.0
    lowest = (theta + corner) / 2.0 - jnp.sqrt(half * half + cross * cross)
    first_weight = corner - lowest
    second_weight = -cross
    size_norm = jnp.sqrt(first_weight * first_weight + second_weight * second_weight + 1e-30)
    entries = (
        lax.axis_size(SECTOR) * lax.axis_size(PAIR) * wavefunction.shape[1] * wavefunction.shape[2]
    )
    scale = jnp.float32(math.sqrt(entries))
    factor_one = scale * first_weight / size_norm
    factor_two = scale * second_weight / size_norm
    new_state = factor_one * vector + factor_two * basis
    new_image = factor_one * image + factor_two * second_image
    energies = jnp.stack([theta, lowest])
    return (new_state, new_image, energies)


def solution(mesh):
    split = Mesh(
        mesh.devices.reshape(2, 4, 4, 4, 2), ("pair_0", "pair_1", "pair_2", "sector_0", "sector_1")
    )
    placed = (
        P(SECTOR, PAIR, None),
        P(SECTOR, PAIR, None),
        P(PAIR, SECTOR, None, None),
        P(PAIR, SECTOR, None, None),
        P(PAIR),
        P(SECTOR, None),
    )
    return jax.shard_map(
        per_device,
        mesh=split,
        in_specs=placed,
        out_specs=(P(SECTOR, PAIR, None), P(SECTOR, PAIR, None), P()),
        check_vma=False,
    )
```

profile of v0, /device:TPU:1, one launch (start us, length us, event | category | flops | bytes accessed | tf_op | source)
XLA Modules:
  0.0 650.0 jit_solution(17976514940221424542)
XLA Ops:
  7.2 4.5 collective-permute-start
  13.0 3.1 collective-permute-done.1
  28.1 128.5 %all-gather.3.cloned.1.call-done = f32[3,512,512]{2,1,0:T(8,128)} async-done(((f32[3,16,512]{2,1,0:T(8,128)}), f32[3,512,512]{2,1,0:T(8,128)}) %all-gather.3.cloned.1.call-update) | async-done | bytes 3145744 | tf_op jit(solution)/shard_map/all_gather | solution.py:23
  156.6 5.2 fusion.78
  162.2 3.5 fusion.21
  165.7 1.9 fusion.68
  167.7 2.2 fusion.23
  169.9 3.9 fusion.66
  173.8 3.5 fusion.18
  179.3 2.2 fusion.25
  181.5 3.7 fusion.54
  185.3 3.5 fusion.14
  189.0 23.1 %collective-permute-start.2 = (f32[512,512]{1,0:T(8,128)S(1)}, f32[512,512]{1,0:T(8,128)S(1)}, u32[]{:S(2)}, u32[]{:S(2)}) collective-permute-start(f32[512,512]{1,0:T(8,128)S(1)} %get-tuple-element.114), channel_id=1, source_target_pairs={{7,0},{0,1},{1,2},{2,3},{3,4},{4,5},{5,6},{6,7},{15,8},{8,9},{9,10... | collective-permute-start | bytes 3145736 | tf_op jit(solution)/shard_map/ppermute | solution.py:17
  214.0 12.9 %collective-permute-done.2 = f32[512,512]{1,0:T(8,128)S(1)} collective-permute-done((f32[512,512]{1,0:T(8,128)S(1)}, f32[512,512]{1,0:T(8,128)S(1)}, u32[]{:S(2)}, u32[]{:S(2)}) %collective-permute-start.2) | collective-permute-done | bytes 1048608 | tf_op jit(solution)/shard_map/ppermute | solution.py:17
  226.9 11.6 %collective-permute-done.3 = f32[512,512]{1,0:T(8,128)S(1)} collective-permute-done((f32[512,512]{1,0:T(8,128)S(1)}, f32[512,512]{1,0:T(8,128)S(1)}, u32[]{:S(2)}, u32[]{:S(2)}) %collective-permute-start.3) | collective-permute-done | bytes 1048608 | tf_op jit(solution)/shard_map/ppermute | solution.py:17
  238.5 2.0 fusion.37
  240.5 21.8 %all_to_all.10 = f32[32,1,16,512]{3,2,1,0:T(8,128)} all-to-all(f32[32,1,16,512]{3,2,1,0:T(8,128)S(1)} %bitcast.225), channel_id=1, replica_groups=mesh['pair_0'=2,'pair_1'=4,'pair_2'=4,'sector_0'=4,'sector_1'=2] {'pair_..., dimensions={0} | all-to-all | bytes 2097152 | tf_op jit(solution)/shard_map/all_to_all | solution.py:35
  264.2 4.5 all-reduce.14
  268.6 9.0 %all-reduce.8 = (f32[]{:T(128)}, f32[]{:T(128)}) all-reduce(f32[]{:T(128)} %get-tuple-element.109, f32[]{:T(128)} %get-tuple-element.110), channel_id=1, replica_groups=mesh['pair_0'=2,'pair_1'=4,'pair_2'=4,'sector_0'=4,'sector_1'=2] {'pair_1'}, use_global_device_ids=true, to_apply=%region_9.10 | all-reduce | flops 2 | bytes 16 | tf_op jit(solution)/shard_map/psum | solution.py:41
  277.7 7.0 %all-reduce.5 = (f32[]{:T(128)}, f32[]{:T(128)}) all-reduce(f32[]{:T(128)} %get-tuple-element.97, f32[]{:T(128)} %get-tuple-element.98), channel_id=1, replica_groups=mesh['pair_0'=2,'pair_1'=4,'pair_2'=4,'sector_0'=4,'sector_1'=2] {'pair_2'}, use_global_device_ids=true, to_apply=%region_10.11 | all-reduce | flops 2 | bytes 16 | tf_op jit(solution)/shard_map/psum | solution.py:41
  284.7 10.7 %all-reduce.2 = (f32[]{:T(128)}, f32[]{:T(128)}) all-reduce(f32[]{:T(128)} %get-tuple-element.91, f32[]{:T(128)} %get-tuple-element.92), channel_id=1, replica_groups=mesh['pair_0'=2,'pair_1'=4,'pair_2'=4,'sector_0'=4,'sector_1'=2] {'secto..., use_global_device_ids=true, to_apply=%region_11.12 | all-reduce | flops 2 | bytes 16 | tf_op jit(solution)/shard_map/psum | solution.py:41
  295.4 10.4 %all-reduce.11 = (f32[]{:T(128)}, f32[]{:T(128)}) all-reduce(f32[]{:T(128)} %get-tuple-element.85, f32[]{:T(128)} %get-tuple-element.86), channel_id=1, replica_groups=mesh['pair_0'=2,'pair_1'=4,'pair_2'=4,'sector_0'=4,'sector_1'=2] {'secto..., use_global_device_ids=true, to_apply=%region_12.13 | all-reduce | flops 2 | bytes 16 | tf_op jit(solution)/shard_map/psum | solution.py:41
  308.5 4.5 all-reduce.13
  313.0 7.8 %all-reduce.7 = (f32[]{:T(128)}, f32[]{:T(128)}) all-reduce(f32[]{:T(128)} %get-tuple-element.107, f32[]{:T(128)} %get-tuple-element.108), channel_id=1, replica_groups=mesh['pair_0'=2,'pair_1'=4,'pair_2'=4,'sector_0'=4,'sector_1'=2] {'pair_1'}, use_global_device_ids=true, to_apply=%region_21.22 | all-reduce | flops 2 | bytes 16 | tf_op jit(solution)/shard_map/psum | solution.py:41
  320.9 6.7 %all-reduce.4 = (f32[]{:T(128)}, f32[]{:T(128)}) all-reduce(f32[]{:T(128)} %get-tuple-element.95, f32[]{:T(128)} %get-tuple-element.96), channel_id=1, replica_groups=mesh['pair_0'=2,'pair_1'=4,'pair_2'=4,'sector_0'=4,'sector_1'=2] {'pair_2'}, use_global_device_ids=true, to_apply=%region_22.23 | all-reduce | flops 2 | bytes 16 | tf_op jit(solution)/shard_map/psum | solution.py:41
  327.5 9.3 %all-reduce.1 = (f32[]{:T(128)}, f32[]{:T(128)}) all-reduce(f32[]{:T(128)} %get-tuple-element.89, f32[]{:T(128)} %get-tuple-element.90), channel_id=1, replica_groups=mesh['pair_0'=2,'pair_1'=4,'pair_2'=4,'sector_0'=4,'sector_1'=2] {'secto..., use_global_device_ids=true, to_apply=%region_23.24 | all-reduce | flops 2 | bytes 16 | tf_op jit(solution)/shard_map/psum | solution.py:41
  336.9 10.1 %all-reduce.10 = (f32[]{:T(128)}, f32[]{:T(128)}) all-reduce(f32[]{:T(128)} %get-tuple-element.83, f32[]{:T(128)} %get-tuple-element.84), channel_id=1, replica_groups=mesh['pair_0'=2,'pair_1'=4,'pair_2'=4,'sector_0'=4,'sector_1'=2] {'secto..., use_global_device_ids=true, to_apply=%region_24.25 | all-reduce | flops 2 | bytes 16 | tf_op jit(solution)/shard_map/psum | solution.py:41
  351.8 3.5 collective-permute-done.5
  356.0 134.3 %all-gather.5.cloned.1.call-done = f32[3,512,512]{2,1,0:T(8,128)} async-done(((f32[3,16,512]{2,1,0:T(8,128)}), f32[3,512,512]{2,1,0:T(8,128)}) %all-gather.5.cloned.1.call-update) | async-done | bytes 3145744 | tf_op jit(solution)/shard_map/all_gather | solution.py:23
  490.2 4.8 fusion.75
  495.5 3.5 fusion.10
  499.0 1.9 fusion.42
  501.0 2.2 fusion.29
  503.2 3.7 fusion.63
  506.9 3.5 fusion.7
  512.4 2.2 fusion.31
  514.6 3.8 fusion.51
  518.4 3.5 fusion.3
  522.1 23.0 %collective-permute-start.6 = (f32[512,512]{1,0:T(8,128)S(1)}, f32[512,512]{1,0:T(8,128)S(1)}, u32[]{:S(2)}, u32[]{:S(2)}) collective-permute-start(f32[512,512]{1,0:T(8,128)S(1)} %get-tuple-element.112), channel_id=1, source_target_pairs={{7,0},{0,1},{1,2},{2,3},{3,4},{4,5},{5,6},{6,7},{15,8},{8,9},{9,10... | collective-permute-start | bytes 3145736 | tf_op jit(solution)/shard_map/ppermute | solution.py:17
  547.0 12.9 %collective-permute-done.6 = f32[512,512]{1,0:T(8,128)S(1)} collective-permute-done((f32[512,512]{1,0:T(8,128)S(1)}, f32[512,512]{1,0:T(8,128)S(1)}, u32[]{:S(2)}, u32[]{:S(2)}) %collective-permute-start.6) | collective-permute-done | bytes 1048608 | tf_op jit(solution)/shard_map/ppermute | solution.py:17
  559.9 11.6 %collective-permute-done.7 = f32[512,512]{1,0:T(8,128)S(1)} collective-permute-done((f32[512,512]{1,0:T(8,128)S(1)}, f32[512,512]{1,0:T(8,128)S(1)}, u32[]{:S(2)}, u32[]{:S(2)}) %collective-permute-start.7) | collective-permute-done | bytes 1048608 | tf_op jit(solution)/shard_map/ppermute | solution.py:17
  571.5 2.0 fusion.35
  573.5 21.8 %all_to_all.11 = f32[32,1,16,512]{3,2,1,0:T(8,128)S(1)} all-to-all(f32[32,1,16,512]{3,2,1,0:T(8,128)S(1)} %bitcast.224), channel_id=1, replica_groups=mesh['pair_0'=2,'pair_1'=4,'pair_2'=4,'sector_0'=4,'sector_1'=2] {'pair_..., dimensions={0} | all-to-all | bytes 2097152 | tf_op jit(solution)/shard_map/all_to_all | solution.py:35
  596.0 4.4 all-reduce.12
  600.4 9.0 %all-reduce.6 = (f32[]{:T(128)}, f32[]{:T(128)}) all-reduce(f32[]{:T(128)} %get-tuple-element.105, f32[]{:T(128)} %get-tuple-element.106), channel_id=1, replica_groups=mesh['pair_0'=2,'pair_1'=4,'pair_2'=4,'sector_0'=4,'sector_1'=2] {'pair_1'}, use_global_device_ids=true, to_apply=%region_34.35 | all-reduce | flops 2 | bytes 16 | tf_op jit(solution)/shard_map/psum | solution.py:41
  609.4 6.9 %all-reduce.3 = (f32[]{:T(128)}, f32[]{:T(128)}) all-reduce(f32[]{:T(128)} %get-tuple-element.93, f32[]{:T(128)} %get-tuple-element.94), channel_id=1, replica_groups=mesh['pair_0'=2,'pair_1'=4,'pair_2'=4,'sector_0'=4,'sector_1'=2] {'pair_2'}, use_global_device_ids=true, to_apply=%region_35.36 | all-reduce | flops 2 | bytes 16 | tf_op jit(solution)/shard_map/psum | solution.py:41
  616.4 10.8 %all-reduce = (f32[]{:T(128)}, f32[]{:T(128)}) all-reduce(f32[]{:T(128)} %get-tuple-element.87, f32[]{:T(128)} %get-tuple-element.88), channel_id=1, replica_groups=mesh['pair_0'=2,'pair_1'=4,'pair_2'=4,'sector_0'=4,'sector_1'=2] {'secto..., use_global_device_ids=true, to_apply=%region_36.37 | all-reduce | flops 2 | bytes 16 | tf_op jit(solution)/shard_map/psum | solution.py:41
  627.1 10.4 %all-reduce.9 = (f32[]{:T(128)}, f32[]{:T(128)}) all-reduce(f32[]{:T(128)} %get-tuple-element.81, f32[]{:T(128)} %get-tuple-element.82), channel_id=1, replica_groups=mesh['pair_0'=2,'pair_1'=4,'pair_2'=4,'sector_0'=4,'sector_1'=2] {'secto..., use_global_device_ids=true, to_apply=%region_37.38 | all-reduce | flops 2 | bytes 16 | tf_op jit(solution)/shard_map/psum | solution.py:41
  (49 shorter events, 22.6 us)
Async XLA Ops:
  7.2 149.5 %all-gather.3.cloned.1.call-start = ((), (), s32[]{:S(2)}) async-start(), calls=%async_computation.2 | async-start | bytes 3244032 | tf_op jit(solution)/shard_map/all_gather | solution.py:23
  7.2 5.8 collective-permute-start
  11.7 4.4 collective-permute-start.1
  17.5 472.7 %all-gather.5.cloned.1.call-start = ((), (), s32[]{:S(2)}) async-start(), calls=%async_computation.3 | async-start | bytes 3244032 | tf_op jit(solution)/shard_map/all_gather | solution.py:23
  156.6 5.6 copy-start.1
  161.8 3.9 copy-start
  161.8 3.9 copy-start.3
  189.0 37.9 %collective-permute-start.2 = (f32[512,512]{1,0:T(8,128)S(1)}, f32[512,512]{1,0:T(8,128)S(1)}, u32[]{:S(2)}, u32[]{:S(2)}) collective-permute-start(f32[512,512]{1,0:T(8,128)S(1)} %get-tuple-element.114), channel_id=1, source_target_pairs={{7,0},{0,1},{1,2},{2,3},{3,4},{4,5},{5,6},{6,7},{15,8},{8,9},{9,10... | collective-permute-start | bytes 3145736 | tf_op jit(solution)/shard_map/ppermute | solution.py:17
  212.0 26.4 %collective-permute-start.3 = (f32[512,512]{1,0:T(8,128)S(1)}, f32[512,512]{1,0:T(8,128)S(1)}, u32[]{:S(2)}, u32[]{:S(2)}) collective-permute-start(f32[512,512]{1,0:T(8,128)S(1)} %get-tuple-element.115), channel_id=1, source_target_pairs={{1,0},{2,1},{3,2},{4,3},{5,4},{6,5},{7,6},{0,7},{9,8},{10,9},{11,1... | collective-permute-start | bytes 3145736 | tf_op jit(solution)/shard_map/ppermute | solution.py:17
  240.4 23.1 %copy-start.5 = (f32[1,16,512]{2,1,0:T(8,128)S(1)}, f32[1,16,512]{2,1,0:T(8,128)}, u32[]{:S(2)}) copy-start(f32[1,16,512]{2,1,0:T(8,128)} %param.18) | copy-start | bytes 98308
  240.4 67.5 %copy-start.6 = (f32[1,16,512]{2,1,0:T(8,128)S(1)}, f32[1,16,512]{2,1,0:T(8,128)}, u32[]{:S(2)}) copy-start(f32[1,16,512]{2,1,0:T(8,128)} %param.19) | copy-start | bytes 98308
  349.6 2.2 collective-permute-start.4
  350.8 4.5 collective-permute-start.5
  490.2 5.3 copy-start.2
  495.1 3.9 copy-start.4
  522.1 37.8 %collective-permute-start.6 = (f32[512,512]{1,0:T(8,128)S(1)}, f32[512,512]{1,0:T(8,128)S(1)}, u32[]{:S(2)}, u32[]{:S(2)}) collective-permute-start(f32[512,512]{1,0:T(8,128)S(1)} %get-tuple-element.112), channel_id=1, source_target_pairs={{7,0},{0,1},{1,2},{2,3},{3,4},{4,5},{5,6},{6,7},{15,8},{8,9},{9,10... | collective-permute-start | bytes 3145736 | tf_op jit(solution)/shard_map/ppermute | solution.py:17
  545.1 26.4 %collective-permute-start.7 = (f32[512,512]{1,0:T(8,128)S(1)}, f32[512,512]{1,0:T(8,128)S(1)}, u32[]{:S(2)}, u32[]{:S(2)}) collective-permute-start(f32[512,512]{1,0:T(8,128)S(1)} %get-tuple-element.113), channel_id=1, source_target_pairs={{1,0},{2,1},{3,2},{4,3},{5,4},{6,5},{7,6},{0,7},{9,8},{10,9},{11,1... | collective-permute-start | bytes 3145736 | tf_op jit(solution)/shard_map/ppermute | solution.py:17
Sparse Core Ops, SparseCore 0:
  17.7 138.9 all-gather.2
  356.1 134.1 all-gather.4
where the time goes:
time: 660 us; the launch traced here: 650 us
  waiting for transfers between devices  321 us (49%)
  blocking collectives  165 us (25%)
  matrix products  70.3 us (11%)
  starting transfers between devices  51.8 us (8%)
  between operations  30.7 us (5%)
  other arithmetic  7.11 us (1%)
    all_gather x2, waiting for transfers between devices, side_by_side(): out = lax.all_gather(both, axis, axis=dim, tiled=True)  263 us
    psum x15, blocking collectives, by_axis(): value = lax.psum(value, axis)  122 us
    dot_general x24, matrix products, product(): jnp.dot(first, second, precision=highest, preferred_element_type=jnp.floa...  70.3 us
    ppermute x8, waiting for transfers between devices, shifted(): return lax.ppermute(block, axis, route)  57.9 us
    ppermute x8, starting transfers between devices, shifted(): return lax.ppermute(block, axis, route)  51.7 us
    all_to_all x2, blocking collectives, sum_at_owner(): lax.all_to_all(cut_along(value, dim, peers), axis, 0, 0, tiled=True)  43.6 us
  transfers between devices with their start and end apart: 10, of which 10 were waited for; matrix products, arithmetic and copies ran while one was open for 1% of the time, Pallas kernels for 0%

commit v1 on v0

--- a/solution.py
+++ b/solution.py
@@ -38,7 +38,8 @@
 
 def by_axis(value, axes):
     for axis in axes:
-        value = lax.psum(value, axis)
+        parts = lax.all_gather(value, axis)
+        value = jnp.sum(parts, axis=0)
     return value
 
 

time: 660 us -> 726 us (1.10)
  local copies, waits for them, and re-layouts: 4.18 us -> 47.7 us
  blocking collectives: 165 us -> 134 us
  other arithmetic: 7.11 us -> 25.8 us
  waiting for transfers between devices: 321 us -> 336 us
  matrix products: 70.3 us -> 83 us
    psum x15 -> x0, blocking collectives: 122 us -> none  [by_axis(): value = lax.psum(value, axis)]
    unnamed x0 -> x15, blocking collectives: none -> 112 us
    unnamed x14 -> x89, local copies, waits for them, and re-layouts: 0.03 us -> 43.6 us
    all_to_all x2 -> x1, blocking collectives: 43.6 us -> 21.8 us  [sum_at_owner(): lax.all_to_all(cut_along(value, dim, peers), axis, 0, 0, tiled=True)]
    reduce_sum x0 -> x30, other arithmetic: none -> 18.5 us  [by_axis(): value = jnp.sum(parts, axis=0)]
    all_to_all x0 -> x1, waiting for transfers between devices: none -> 15.2 us  [sum_at_owner(): lax.all_to_all(cut_along(value, dim, peers), axis, 0, 0, tiled=True)]
    dot_general x24, matrix products: 70.3 us -> 83 us  [product(): jnp.dot(first, second, precision=highest, preferred_element_type=jnp.floa...]
  transfers between devices with their start and end apart: 10 -> 11, of which waited for: 10 -> 11; matrix products, arithmetic and copies ran while one was open for 1% -> 1% of each run, Pallas kernels for 0% -> 0%
where the time goes in v1:
time: 726 us; the launch traced here: 715 us
  waiting for transfers between devices  336 us (46%)
  blocking collectives  134 us (18%)
  matrix products  83 us (11%)
  starting transfers between devices  58.1 us (8%)
  local copies, waits for them, and re-layouts  47.7 us (7%)
  between operations  30.8 us (4%)
  other arithmetic  25.8 us (4%)
    all_gather x2, waiting for transfers between devices, side_by_side(): out = lax.all_gather(both, axis, axis=dim, tiled=True)  263 us
    unnamed x15, blocking collectives  112 us
    dot_general x24, matrix products, product(): jnp.dot(first, second, precision=highest, preferred_element_type=jnp.floa...  83 us
    ppermute x8, waiting for transfers between devices, shifted(): return lax.ppermute(block, axis, route)  57.7 us
    ppermute x8, starting transfers between devices, shifted(): return lax.ppermute(block, axis, route)  51.7 us
    unnamed x89, local copies, waits for them, and re-layouts  43.6 us
    all_to_all x1, blocking collectives, sum_at_owner(): lax.all_to_all(cut_along(value, dim, peers), axis, 0, 0, tiled=True)  21.8 us
    reduce_sum x30, other arithmetic, by_axis(): value = jnp.sum(parts, axis=0)  18.5 us
  transfers between devices with their start and end apart: 11, of which 11 were waited for; matrix products, arithmetic and copies ran while one was open for 1% of the time, Pallas kernels for 0%

profile of v1, /device:TPU:1, one launch (start us, length us, event | category | flops | bytes accessed | tf_op | source)
XLA Modules:
  0.0 715.2 jit_solution(2061353207486023864)
XLA Ops:
  7.2 4.5 collective-permute-start
  13.0 3.1 collective-permute-done.1
  28.0 128.6 %all-gather.3.cloned.1.call-done = f32[3,512,512]{2,1,0:T(8,128)} async-done(((f32[3,16,512]{2,1,0:T(8,128)}), f32[3,512,512]{2,1,0:T(8,128)}) %all-gather.3.cloned.1.call-update) | async-done | bytes 3145744 | tf_op jit(solution)/shard_map/all_gather | solution.py:23
  156.6 5.2 fusion.78
  162.2 3.5 fusion.21
  167.7 2.2 fusion.23
  169.9 3.8 fusion.66
  173.8 3.5 fusion.18
  179.2 2.2 fusion.25
  181.4 15.5 %fusion.54 = f32[512,512]{1,0:T(8,128)S(1)} fusion(f32[3,512,512]{2,1,0:T(8,128)S(1)} %copy-done.3, f32[3,1,512,512]{3,2,1,0:T(8,128)S(1)} %copy-done), kind=kOutput, calls=%fused_computation.72 | convolution fusion | flops 1610612736 | bytes 3145728 | tf_op jit(solution)/shard_map/dot_general | solution.py:47
  196.9 3.5 fusion.14
  200.6 23.0 %collective-permute-start.2 = (f32[512,512]{1,0:T(8,128)S(1)}, f32[512,512]{1,0:T(8,128)S(1)}, u32[]{:S(2)}, u32[]{:S(2)}) collective-permute-start(f32[512,512]{1,0:T(8,128)S(1)} %get-tuple-element.114), channel_id=1, source_target_pairs={{7,0},{0,1},{1,2},{2,3},{3,4},{4,5},{5,6},{6,7},{15,8},{8,9},{9,10... | collective-permute-start | bytes 3145736 | tf_op jit(solution)/shard_map/ppermute | solution.py:17
  225.6 12.9 %collective-permute-done.2 = f32[512,512]{1,0:T(8,128)S(1)} collective-permute-done((f32[512,512]{1,0:T(8,128)S(1)}, f32[512,512]{1,0:T(8,128)S(1)}, u32[]{:S(2)}, u32[]{:S(2)}) %collective-permute-start.2) | collective-permute-done | bytes 1048608 | tf_op jit(solution)/shard_map/ppermute | solution.py:17
  238.4 11.7 %collective-permute-done.3 = f32[512,512]{1,0:T(8,128)S(1)} collective-permute-done((f32[512,512]{1,0:T(8,128)S(1)}, f32[512,512]{1,0:T(8,128)S(1)}, u32[]{:S(2)}, u32[]{:S(2)}) %collective-permute-start.3) | collective-permute-done | bytes 1048608 | tf_op jit(solution)/shard_map/ppermute | solution.py:17
  250.1 3.1 fusion.37
  253.2 6.4 all-to-all-start
  260.2 15.2 %all-to-all-done = f32[32,1,16,512]{3,2,1,0:T(8,128)} async-done(((f32[32,1,16,512]{3,2,1,0:T(8,128)}), f32[32,1,16,512]{3,2,1,0:T(8,128)}, u32[]{:S(2)}, u32[]{:S(2)}) %all-to-all-start) | async-done | bytes 1048608 | tf_op jit(solution)/shard_map/all_to_all | solution.py:35
  280.7 3.8 all-reduce.44
  289.0 8.4 %all-reduce.38 = (f32[4]{0:T(128)S(1)}, f32[4]{0:T(128)S(1)}) all-reduce(f32[4]{0:T(128)S(1)} %dynamic-update-slice.24, f32[4]{0:T(128)S(1)} %dynamic-update-slice.19), channel_id=1, replica_groups=mesh['pair_0'=2,'pair_1'=4,'pair_2'=4,'sector_0'=4,'sector_1'=2] {'pair_1'}, use_global_device_ids=true, to_apply=%add.6 | all-reduce | flops 8 | bytes 64
  302.1 6.3 all-reduce.35
  313.1 10.1 %all-reduce.32 = (f32[4]{0:T(128)S(1)}, f32[4]{0:T(128)S(1)}) all-reduce(f32[4]{0:T(128)S(1)} %dynamic-update-slice.26, f32[4]{0:T(128)S(1)} %dynamic-update-slice.21), channel_id=1, replica_groups=mesh['pair_0'=2,'pair_1'=4,'pair_2'=4,'sector_0'=4,'sector_1'=2] {'secto..., use_global_device_ids=true, to_apply=%add.8 | all-reduce | flops 8 | bytes 64
  327.1 9.7 %all-reduce.41 = (f32[2]{0:T(128)S(1)}, f32[2]{0:T(128)S(1)}) all-reduce(f32[2]{0:T(128)S(1)} %dynamic-update-slice.27, f32[2]{0:T(128)S(1)} %dynamic-update-slice.22), channel_id=1, replica_groups=mesh['pair_0'=2,'pair_1'=4,'pair_2'=4,'sector_0'=4,'sector_1'=2] {'secto..., use_global_device_ids=true, to_apply=%add.9 | all-reduce | flops 4 | bytes 32
  343.5 3.8 all-reduce.43
  351.1 7.2 %all-reduce.37 = (f32[4]{0:T(128)S(1)}, f32[4]{0:T(128)S(1)}) all-reduce(f32[4]{0:T(128)S(1)} %dynamic-update-slice.34, f32[4]{0:T(128)S(1)} %dynamic-update-slice.29), channel_id=1, replica_groups=mesh['pair_0'=2,'pair_1'=4,'pair_2'=4,'sector_0'=4,'sector_1'=2] {'pair_1'}, use_global_device_ids=true, to_apply=%add.16 | all-reduce | flops 8 | bytes 64
  362.3 6.0 all-reduce.34
  372.3 8.6 %all-reduce.31 = (f32[4]{0:T(128)S(1)}, f32[4]{0:T(128)S(1)}) all-reduce(f32[4]{0:T(128)S(1)} %dynamic-update-slice.36, f32[4]{0:T(128)S(1)} %dynamic-update-slice.31), channel_id=1, replica_groups=mesh['pair_0'=2,'pair_1'=4,'pair_2'=4,'sector_0'=4,'sector_1'=2] {'secto..., use_global_device_ids=true, to_apply=%add.18 | all-reduce | flops 8 | bytes 64
  384.7 9.4 %all-reduce.40 = (f32[2]{0:T(128)S(1)}, f32[2]{0:T(128)S(1)}) all-reduce(f32[2]{0:T(128)S(1)} %dynamic-update-slice.37, f32[2]{0:T(128)S(1)} %dynamic-update-slice.32), channel_id=1, replica_groups=mesh['pair_0'=2,'pair_1'=4,'pair_2'=4,'sector_0'=4,'sector_1'=2] {'secto..., use_global_device_ids=true, to_apply=%add.19 | all-reduce | flops 4 | bytes 32
  400.0 3.7 collective-permute-done.5
  404.3 134.5 %all-gather.5.cloned.1.call-done = f32[3,512,512]{2,1,0:T(8,128)} async-done(((f32[3,16,512]{2,1,0:T(8,128)}), f32[3,512,512]{2,1,0:T(8,128)}) %all-gather.5.cloned.1.call-update) | async-done | bytes 3145744 | tf_op jit(solution)/shard_map/all_gather | solution.py:23
  538.8 4.8 fusion.75
  544.1 3.5 fusion.10
  549.5 2.2 fusion.29
  551.7 3.7 fusion.63
  555.5 3.5 fusion.7
  559.0 1.9 fusion.40
  560.9 2.2 fusion.31
  563.2 3.8 fusion.51
  567.0 3.5 fusion.3
  570.6 23.0 %collective-permute-start.6 = (f32[512,512]{1,0:T(8,128)S(1)}, f32[512,512]{1,0:T(8,128)S(1)}, u32[]{:S(2)}, u32[]{:S(2)}) collective-permute-start(f32[512,512]{1,0:T(8,128)S(1)} %get-tuple-element.112), channel_id=1, source_target_pairs={{7,0},{0,1},{1,2},{2,3},{3,4},{4,5},{5,6},{6,7},{15,8},{8,9},{9,10... | collective-permute-start | bytes 3145736 | tf_op jit(solution)/shard_map/ppermute | solution.py:17
  595.6 12.9 %collective-permute-done.6 = f32[512,512]{1,0:T(8,128)S(1)} collective-permute-done((f32[512,512]{1,0:T(8,128)S(1)}, f32[512,512]{1,0:T(8,128)S(1)}, u32[]{:S(2)}, u32[]{:S(2)}) %collective-permute-start.6) | collective-permute-done | bytes 1048608 | tf_op jit(solution)/shard_map/ppermute | solution.py:17
  608.4 11.6 %collective-permute-done.7 = f32[512,512]{1,0:T(8,128)S(1)} collective-permute-done((f32[512,512]{1,0:T(8,128)S(1)}, f32[512,512]{1,0:T(8,128)S(1)}, u32[]{:S(2)}, u32[]{:S(2)}) %collective-permute-start.7) | collective-permute-done | bytes 1048608 | tf_op jit(solution)/shard_map/ppermute | solution.py:17
  620.0 2.0 fusion.35
  622.1 21.8 %all_to_all.10 = f32[32,1,16,512]{3,2,1,0:T(8,128)S(1)} all-to-all(f32[32,1,16,512]{3,2,1,0:T(8,128)S(1)} %bitcast.260), channel_id=1, replica_groups=mesh['pair_0'=2,'pair_1'=4,'pair_2'=4,'sector_0'=4,'sector_1'=2] {'pair_..., dimensions={0} | all-to-all | bytes 2097152 | tf_op jit(solution)/shard_map/all_to_all | solution.py:35
  647.2 3.8 all-reduce.42
  654.8 8.4 %all-reduce.36 = (f32[4]{0:T(128)S(1)}, f32[4]{0:T(128)S(1)}) all-reduce(f32[4]{0:T(128)S(1)} %dynamic-update-slice.44, f32[4]{0:T(128)S(1)} %dynamic-update-slice.39), channel_id=1, replica_groups=mesh['pair_0'=2,'pair_1'=4,'pair_2'=4,'sector_0'=4,'sector_1'=2] {'pair_1'}, use_global_device_ids=true, to_apply=%add.26 | all-reduce | flops 8 | bytes 64
  667.2 6.3 all-reduce.33
  677.4 10.0 %all-reduce.30 = (f32[4]{0:T(128)S(1)}, f32[4]{0:T(128)S(1)}) all-reduce(f32[4]{0:T(128)S(1)} %dynamic-update-slice.46, f32[4]{0:T(128)S(1)} %dynamic-update-slice.41), channel_id=1, replica_groups=mesh['pair_0'=2,'pair_1'=4,'pair_2'=4,'sector_0'=4,'sector_1'=2] {'secto..., use_global_device_ids=true, to_apply=%add.28 | all-reduce | flops 8 | bytes 64
  691.3 10.2 %all-reduce.39 = (f32[2]{0:T(128)S(1)}, f32[2]{0:T(128)S(1)}) all-reduce(f32[2]{0:T(128)S(1)} %dynamic-update-slice.47, f32[2]{0:T(128)S(1)} %dynamic-update-slice.42), channel_id=1, replica_groups=mesh['pair_0'=2,'pair_1'=4,'pair_2'=4,'sector_0'=4,'sector_1'=2] {'secto..., use_global_device_ids=true, to_apply=%add.29 | all-reduce | flops 4 | bytes 32
  (155 shorter events, 86.4 us)
Async XLA Ops:
  7.2 149.5 %all-gather.3.cloned.1.call-start = ((), (), s32[]{:S(2)}) async-start(), calls=%async_computation.2 | async-start | bytes 3244032 | tf_op jit(solution)/shard_map/all_gather | solution.py:23
  7.2 5.8 collective-permute-start
  11.7 4.4 collective-permute-start.1
  156.6 5.6 copy-start.1
  161.8 3.9 copy-start
  161.8 3.9 copy-start.3
  200.6 37.8 %collective-permute-start.2 = (f32[512,512]{1,0:T(8,128)S(1)}, f32[512,512]{1,0:T(8,128)S(1)}, u32[]{:S(2)}, u32[]{:S(2)}) collective-permute-start(f32[512,512]{1,0:T(8,128)S(1)} %get-tuple-element.114), channel_id=1, source_target_pairs={{7,0},{0,1},{1,2},{2,3},{3,4},{4,5},{5,6},{6,7},{15,8},{8,9},{9,10... | collective-permute-start | bytes 3145736 | tf_op jit(solution)/shard_map/ppermute | solution.py:17
  223.6 26.5 %collective-permute-start.3 = (f32[512,512]{1,0:T(8,128)S(1)}, f32[512,512]{1,0:T(8,128)S(1)}, u32[]{:S(2)}, u32[]{:S(2)}) collective-permute-start(f32[512,512]{1,0:T(8,128)S(1)} %get-tuple-element.115), channel_id=1, source_target_pairs={{1,0},{2,1},{3,2},{4,3},{5,4},{6,5},{7,6},{0,7},{9,8},{10,9},{11,1... | collective-permute-start | bytes 3145736 | tf_op jit(solution)/shard_map/ppermute | solution.py:17
  225.6 34.1 %copy-start.11 = (u32[256]{0:T(256)S(1)}, u32[256]{0:T(256)}, u32[]{:S(2)}) copy-start(u32[256]{0:T(256)} %constant.208) | copy-start | bytes 3076
  253.2 23.5 %copy-start.5 = (f32[1,16,512]{2,1,0:T(8,128)S(1)}, f32[1,16,512]{2,1,0:T(8,128)}, u32[]{:S(2)}) copy-start(f32[1,16,512]{2,1,0:T(8,128)} %param.18) | copy-start | bytes 98308
  253.2 26.9 %copy-start.10 = (u32[256]{0:T(256)S(1)}, u32[256]{0:T(256)}, u32[]{:S(2)}) copy-start(u32[256]{0:T(256)} %constant.213) | copy-start | bytes 3076
  253.2 35.2 %copy-start.9 = (u32[256]{0:T(256)S(1)}, u32[256]{0:T(256)}, u32[]{:S(2)}) copy-start(u32[256]{0:T(256)} %constant.218) | copy-start | bytes 3076
  253.2 48.3 %copy-start.8 = (u32[256]{0:T(256)S(1)}, u32[256]{0:T(256)}, u32[]{:S(2)}) copy-start(u32[256]{0:T(256)} %constant.223) | copy-start | bytes 3076
  253.2 59.3 %copy-start.7 = (u32[256]{0:T(256)S(1)}, u32[256]{0:T(256)}, u32[]{:S(2)}) copy-start(u32[256]{0:T(256)} %constant.228) | copy-start | bytes 3076
  253.2 86.9 %copy-start.6 = (f32[1,16,512]{2,1,0:T(8,128)S(1)}, f32[1,16,512]{2,1,0:T(8,128)}, u32[]{:S(2)}) copy-start(f32[1,16,512]{2,1,0:T(8,128)} %param.19) | copy-start | bytes 98308
  253.2 22.2 %all-to-all-start = ((f32[32,1,16,512]{3,2,1,0:T(8,128)}), f32[32,1,16,512]{3,2,1,0:T(8,128)}, u32[]{:S(2)}, u32[]{:S(2)}) async-start(f32[32,1,16,512]{3,2,1,0:T(8,128)} %bitcast.259), calls=%async_computation | async-start | bytes 2097152 | tf_op jit(solution)/shard_map/all_to_all | solution.py:35
  259.6 279.2 %all-gather.5.cloned.1.call-start = ((), (), s32[]{:S(2)}) async-start(), calls=%async_computation.3 | async-start | bytes 3244032 | tf_op jit(solution)/shard_map/all_gather | solution.py:23
  398.2 1.8 collective-permute-start.4
  399.0 4.7 collective-permute-start.5
  538.8 5.3 copy-start.2
  543.6 3.9 copy-start.4
  570.6 37.8 %collective-permute-start.6 = (f32[512,512]{1,0:T(8,128)S(1)}, f32[512,512]{1,0:T(8,128)S(1)}, u32[]{:S(2)}, u32[]{:S(2)}) collective-permute-start(f32[512,512]{1,0:T(8,128)S(1)} %get-tuple-element.112), channel_id=1, source_target_pairs={{7,0},{0,1},{1,2},{2,3},{3,4},{4,5},{5,6},{6,7},{15,8},{8,9},{9,10... | collective-permute-start | bytes 3145736 | tf_op jit(solution)/shard_map/ppermute | solution.py:17
  593.7 26.4 %collective-permute-start.7 = (f32[512,512]{1,0:T(8,128)S(1)}, f32[512,512]{1,0:T(8,128)S(1)}, u32[]{:S(2)}, u32[]{:S(2)}) collective-permute-start(f32[512,512]{1,0:T(8,128)S(1)} %get-tuple-element.113), channel_id=1, source_target_pairs={{1,0},{2,1},{3,2},{4,3},{5,4},{6,5},{7,6},{0,7},{9,8},{10,9},{11,1... | collective-permute-start | bytes 3145736 | tf_op jit(solution)/shard_map/ppermute | solution.py:17
Sparse Core Ops, SparseCore 0:
  17.7 138.9 all-gather.2
  404.4 134.2 all-gather.4
